TPU v7x, 256 devices: a whole 4x4x8 slice. The times are simulated.
256 devices in a mesh: sweep: 8 (over y, core), layer: 32 (over z, x).
Axes of the slice: x: 4, y: 4, z: 8, core: 2. Of those that a mesh axis runs over, the one named last changes fastest.
Arguments:
- face_rhs: float32 [8, 16, 128, 384], P('sweep', None, 'layer'), may hold values from -6 to 6
- res_rows: float32 [131072, 384], P(('sweep', 'layer')), may hold values from -4 to 4
- row_owner: int32 [131072, 1], P(('sweep', 'layer')), may hold values from 0 to 31; in each aligned block of 512 rows (0 to 511, 512 to 1023, ...) at most 32 rows name the same one
- row_slot: int32 [131072], P(('sweep', 'layer')), may hold values from 0 to 63
- inv_blocks: bfloat16 [8, 128, 384, 384], P('sweep', 'layer'), may hold values from -0.3125 to 0.3125
- couple_in: bfloat16 [8, 1536, 49152], P('sweep', None, 'layer'), may hold values from -0.15625 to 0.15625
- couple_out: bfloat16 [8, 49152, 1536], P('sweep', 'layer'), may hold values from -0.02734375 to 0.02734375
Outputs:
- solved: float32 [8, 16, 128, 384], P('sweep', None, 'layer')
Inputs may be any that keep to these rules, and one draw needn't show every extreme that they name: `row_owner`: among the 512 rows of one device no owner is named by more than 32 rows, a bound that some block reaches.
All inputs are finite; a program needn't handle non-finite values.
Results may differ from a plain program's by a relative error of at most 0.02.
Values may be sent and summed in bfloat16 or wider, within the bound.
No kernel may reach another device: no remote copies, remote signals or barrier semaphores. Data moves between devices by JAX's collectives and lax.ppermute only.
A program may use at most 64 MiB of HBM per device.

v0:
```python
import jax
import jax.numpy as jnp
from jax import lax
from jax.sharding import PartitionSpec as P


def shifted(block, axis, distance):
    devices = range(lax.axis_size(axis))
    route = [(i - distance, i) for i in devices if i - distance in devices]
    return lax.ppermute(block, axis, route)


def on_device(face_rhs, res_rows, row_owner, row_slot, inv_blocks, couple_in, couple_out):
    group_size = lax.axis_size("layer")
    rhs_count = face_rhs.shape[1]
    face_dev = face_rhs.shape[2]
    face_width = face_rhs.shape[3]
    slot_count = rhs_count * face_dev
    row_total = res_rows.shape[0]
    owners = row_owner[:, 0]
    capacity = 2 * row_total // group_size
    matches = (owners[:, None] == jnp.arange(group_size, dtype=jnp.int32)[None, :]).astype(
        jnp.int32
    )
    earlier = jnp.cumsum(matches, axis=0) - matches
    position = jnp.sum(earlier * matches, axis=1)
    destination = owners * capacity + position
    send_rows = (
        jnp.zeros((group_size * capacity, face_width), jnp.float32).at[destination].set(res_rows)
    )
    send_slots = jnp.full((group_size * capacity,), -1, jnp.int32).at[destination].set(row_slot)
    got_rows, got_slots = (
        lax.all_to_all(
            send_rows.reshape(group_size, capacity, face_width),
            "layer",
            split_axis=0,
            concat_axis=0,
            tiled=True,
        ),
        lax.all_to_all(
            send_slots.reshape(group_size, capacity),
            "layer",
            split_axis=0,
            concat_axis=0,
            tiled=True,
        ),
    )
    one_hot = (jnp.arange(slot_count, dtype=jnp.int32)[:, None] == got_slots.reshape(1, -1)).astype(
        jnp.float32
    )
    added_rows = jnp.dot(one_hot, got_rows.reshape(-1, face_width), precision=lax.Precision.HIGHEST)
    assembled = face_rhs[0] + added_rows.reshape(rhs_count, face_dev, face_width)
    coupling_in = couple_in[0]
    coupling_out = couple_out[0]
    inverse = inv_blocks[0]
    sections = lax.axis_size("sweep")
    panel_in = jnp.zeros((rhs_count, coupling_in.shape[0]), jnp.bfloat16)
    solved = jnp.zeros_like(assembled)
    panel_part = jnp.zeros((rhs_count, coupling_in.shape[0]), jnp.float32)
    for step_index in range(sections):
        coupled = jnp.dot(panel_in, coupling_in, preferred_element_type=jnp.float32)
        local_part = (assembled - coupled.reshape(rhs_count, face_dev, face_width)).astype(
            jnp.bfloat16
        )
        solve_solved = jnp.einsum(
            "rfw,fwv->rfv", local_part, inverse, preferred_element_type=jnp.float32
        )
        flattened = solve_solved.astype(jnp.bfloat16).reshape(rhs_count, face_dev * face_width)
        solve_panel_part = jnp.dot(flattened, coupling_out, preferred_element_type=jnp.float32)
        solved = solve_solved
        panel_part = solve_panel_part
        if step_index + 1 < sections:
            summed = lax.psum(panel_part, "layer").astype(jnp.bfloat16)
            arrived = shifted(summed, "sweep", 1)
            panel_in = arrived
    return solved[None]


def solution(mesh):
    return jax.shard_map(
        on_device,
        mesh=mesh,
        in_specs=(
            P("sweep", None, "layer", None),
            P(("sweep", "layer"), None),
            P(("sweep", "layer"), None),
            P(("sweep", "layer")),
            P("sweep", "layer", None, None),
            P("sweep", None, "layer"),
            P("sweep", "layer", None),
        ),
        out_specs=P("sweep", None, "layer", None),
        check_vma=False,
    )
```

profile of v0, /device:TPU:1, one launch (start us, length us, event | category | flops | bytes accessed | tf_op | source)
XLA Modules:
  0.0 1123.9 jit_solution(9724480542182899194)
XLA Ops:
  0.0 0.8 fusion.171
  0.8 1.2 reduce-window.6
  2.2 0.8 fusion.170
  3.0 0.7 compare_select_fusion
  3.7 2.6 scatter_custom_fusion
  7.0 11.9 %all-to-all-start = ((s32[32,1,32]{2,1,0:T(1,128)}), s32[32,1,32]{2,1,0:T(1,128)S(1)}, u32[]{:S(2)}, u32[]{:S(2)}) async-start(s32[32,1,32]{2,1,0:T(1,128)} %all_to_all.9), calls=%async_computation | async-start | bytes 32768 | tf_op jit(solution)/shard_map/all_to_all | solution.py:40
  18.9 4.0 scatter_custom_fusion.1
  22.9 4.5 all-to-all-done
  27.4 4.7 all-to-all-start.1
  33.4 35.1 %all-to-all-done.1 = f32[32,32,384]{2,1,0:T(8,128)S(1)} async-done(((f32[32,32,384]{2,1,0:T(8,128)}), f32[32,32,384]{2,1,0:T(8,128)S(1)}, u32[]{:S(2)}, u32[]{:S(2)}) %all-to-all-start.1) | async-done | bytes 1572896 | tf_op jit(solution)/shard_map/all_to_all | solution.py:33
  68.5 0.7 convolution_add_fusion
  69.2 3.2 fusion.136
  72.4 3.1 fusion.28
  75.5 112.3 %psum.49 = bf16[16,1536]{1,0:T(8,128)(2,1)S(1)} all-reduce(f32[16,1536]{1,0:T(8,128)S(1)} %fusion.28), channel_id=1, replica_groups=mesh['sweep'=8,'layer'=32] {'layer'}, use_global_device_ids=true, to_apply=%region_5.6 | all-reduce | flops 24576 | bytes 147456 | tf_op jit(solution)/shard_map/psum | solution.py:73
  187.8 34.2 %collective-permute-start = (bf16[16,1536]{1,0:T(8,128)(2,1)S(1)}, bf16[16,1536]{1,0:T(8,128)(2,1)S(1)}, u32[]{:S(2)}, u32[]{:S(2)}) collective-permute-start(bf16[16,1536]{1,0:T(8,128)(2,1)S(1)} %psum.49), channel_id=1, source_target_pairs={{0,32},{32,64},{64,96},{96,128},{128,160},{160,192},{192,224},{1,3... | collective-permute-start | bytes 147464 | tf_op jit(solution)/shard_map/ppermute | solution.py:10
  222.0 1.2 collective-permute-done
  223.2 3.2 fusion.133
  226.4 3.1 fusion.26
  229.5 110.7 %psum.50 = bf16[16,1536]{1,0:T(8,128)(2,1)S(1)} all-reduce(f32[16,1536]{1,0:T(8,128)S(1)} %fusion.26), channel_id=1, replica_groups=mesh['sweep'=8,'layer'=32] {'layer'}, use_global_device_ids=true, to_apply=%region_6.7 | all-reduce | flops 24576 | bytes 147456 | tf_op jit(solution)/shard_map/psum | solution.py:73
  340.2 31.3 %collective-permute-start.1 = (bf16[16,1536]{1,0:T(8,128)(2,1)S(1)}, bf16[16,1536]{1,0:T(8,128)(2,1)S(1)}, u32[]{:S(2)}, u32[]{:S(2)}) collective-permute-start(bf16[16,1536]{1,0:T(8,128)(2,1)S(1)} %psum.50), channel_id=1, source_target_pairs={{0,32},{32,64},{64,96},{96,128},{128,160},{160,192},{192,224},{1,3... | collective-permute-start | bytes 147464 | tf_op jit(solution)/shard_map/ppermute | solution.py:10
  371.5 1.2 collective-permute-done.1
  372.6 3.2 fusion.130
  375.9 3.1 fusion.24
  378.9 110.1 %psum.51 = bf16[16,1536]{1,0:T(8,128)(2,1)S(1)} all-reduce(f32[16,1536]{1,0:T(8,128)S(1)} %fusion.24), channel_id=1, replica_groups=mesh['sweep'=8,'layer'=32] {'layer'}, use_global_device_ids=true, to_apply=%region_7.8 | all-reduce | flops 24576 | bytes 147456 | tf_op jit(solution)/shard_map/psum | solution.py:73
  489.0 31.9 %collective-permute-start.2 = (bf16[16,1536]{1,0:T(8,128)(2,1)S(1)}, bf16[16,1536]{1,0:T(8,128)(2,1)S(1)}, u32[]{:S(2)}, u32[]{:S(2)}) collective-permute-start(bf16[16,1536]{1,0:T(8,128)(2,1)S(1)} %psum.51), channel_id=1, source_target_pairs={{0,32},{32,64},{64,96},{96,128},{128,160},{160,192},{192,224},{1,3... | collective-permute-start | bytes 147464 | tf_op jit(solution)/shard_map/ppermute | solution.py:10
  520.9 1.2 collective-permute-done.2
  522.1 3.2 fusion.127
  525.3 3.1 fusion.22
  528.4 110.1 %psum.52 = bf16[16,1536]{1,0:T(8,128)(2,1)S(1)} all-reduce(f32[16,1536]{1,0:T(8,128)S(1)} %fusion.22), channel_id=1, replica_groups=mesh['sweep'=8,'layer'=32] {'layer'}, use_global_device_ids=true, to_apply=%region_8.9 | all-reduce | flops 24576 | bytes 147456 | tf_op jit(solution)/shard_map/psum | solution.py:73
  638.6 32.0 %collective-permute-start.3 = (bf16[16,1536]{1,0:T(8,128)(2,1)S(1)}, bf16[16,1536]{1,0:T(8,128)(2,1)S(1)}, u32[]{:S(2)}, u32[]{:S(2)}) collective-permute-start(bf16[16,1536]{1,0:T(8,128)(2,1)S(1)} %psum.52), channel_id=1, source_target_pairs={{0,32},{32,64},{64,96},{96,128},{128,160},{160,192},{192,224},{1,3... | collective-permute-start | bytes 147464 | tf_op jit(solution)/shard_map/ppermute | solution.py:10
  670.6 1.0 collective-permute-done.3
  671.6 3.2 fusion.124
  674.8 3.1 fusion.20
  677.9 110.4 %psum.53 = bf16[16,1536]{1,0:T(8,128)(2,1)S(1)} all-reduce(f32[16,1536]{1,0:T(8,128)S(1)} %fusion.20), channel_id=1, replica_groups=mesh['sweep'=8,'layer'=32] {'layer'}, use_global_device_ids=true, to_apply=%region_9.10 | all-reduce | flops 24576 | bytes 147456 | tf_op jit(solution)/shard_map/psum | solution.py:73
  788.2 31.6 %collective-permute-start.4 = (bf16[16,1536]{1,0:T(8,128)(2,1)S(1)}, bf16[16,1536]{1,0:T(8,128)(2,1)S(1)}, u32[]{:S(2)}, u32[]{:S(2)}) collective-permute-start(bf16[16,1536]{1,0:T(8,128)(2,1)S(1)} %psum.53), channel_id=1, source_target_pairs={{0,32},{32,64},{64,96},{96,128},{128,160},{160,192},{192,224},{1,3... | collective-permute-start | bytes 147464 | tf_op jit(solution)/shard_map/ppermute | solution.py:10
  819.9 1.2 collective-permute-done.4
  821.0 3.2 fusion.121
  824.3 3.1 fusion.18
  827.3 110.5 %psum.54 = bf16[16,1536]{1,0:T(8,128)(2,1)S(1)} all-reduce(f32[16,1536]{1,0:T(8,128)S(1)} %fusion.18), channel_id=1, replica_groups=mesh['sweep'=8,'layer'=32] {'layer'}, use_global_device_ids=true, to_apply=%region_10.11 | all-reduce | flops 24576 | bytes 147456 | tf_op jit(solution)/shard_map/psum | solution.py:73
  937.8 31.5 %collective-permute-start.5 = (bf16[16,1536]{1,0:T(8,128)(2,1)S(1)}, bf16[16,1536]{1,0:T(8,128)(2,1)S(1)}, u32[]{:S(2)}, u32[]{:S(2)}) collective-permute-start(bf16[16,1536]{1,0:T(8,128)(2,1)S(1)} %psum.54), channel_id=1, source_target_pairs={{0,32},{32,64},{64,96},{96,128},{128,160},{160,192},{192,224},{1,3... | collective-permute-start | bytes 147464 | tf_op jit(solution)/shard_map/ppermute | solution.py:10
  969.3 1.2 collective-permute-done.5
  970.5 3.2 fusion.118
  973.7 3.1 fusion.16
  976.8 110.7 %psum.55 = bf16[16,1536]{1,0:T(8,128)(2,1)S(1)} all-reduce(f32[16,1536]{1,0:T(8,128)S(1)} %fusion.16), channel_id=1, replica_groups=mesh['sweep'=8,'layer'=32] {'layer'}, use_global_device_ids=true, to_apply=%region_11.12 | all-reduce | flops 24576 | bytes 147456 | tf_op jit(solution)/shard_map/psum | solution.py:73
  1087.4 31.3 %collective-permute-start.6 = (bf16[16,1536]{1,0:T(8,128)(2,1)S(1)}, bf16[16,1536]{1,0:T(8,128)(2,1)S(1)}, u32[]{:S(2)}, u32[]{:S(2)}) collective-permute-start(bf16[16,1536]{1,0:T(8,128)(2,1)S(1)} %psum.55), channel_id=1, source_target_pairs={{0,32},{32,64},{64,96},{96,128},{128,160},{160,192},{192,224},{1,3... | collective-permute-start | bytes 147464 | tf_op jit(solution)/shard_map/ppermute | solution.py:10
  1118.8 1.2 collective-permute-done.6
  1120.0 3.2 fusion.46
  1123.2 0.7 copy.19
  (19 shorter events, 2.3 us)
Async XLA Ops:
  0.0 69.2 %copy-start = (bf16[1,4,384,384]{3,2,1,0:T(8,128)(2,1)S(1)}, bf16[1,4,384,384]{3,2,1,0:T(8,128)(2,1)}, u32[]{:S(2)}) copy-start(bf16[1,4,384,384]{3,2,1,0:T(8,128)(2,1)} %param.11) | copy-start | bytes 3538948
  0.0 68.5 %copy-start.1 = (f32[1,16,4,384]{3,2,1,0:T(4,128)S(1)}, f32[1,16,4,384]{3,2,1,0:T(4,128)}, u32[]{:S(2)}) copy-start(f32[1,16,4,384]{3,2,1,0:T(4,128)} %param.7) | copy-start | bytes 294916
  7.0 20.4 %all-to-all-start = ((s32[32,1,32]{2,1,0:T(1,128)}), s32[32,1,32]{2,1,0:T(1,128)S(1)}, u32[]{:S(2)}, u32[]{:S(2)}) async-start(s32[32,1,32]{2,1,0:T(1,128)} %all_to_all.9), calls=%async_computation | async-start | bytes 32768 | tf_op jit(solution)/shard_map/all_to_all | solution.py:40
  27.4 41.1 %all-to-all-start.1 = ((f32[32,32,384]{2,1,0:T(8,128)}), f32[32,32,384]{2,1,0:T(8,128)S(1)}, u32[]{:S(2)}, u32[]{:S(2)}) async-start(f32[32,32,384]{2,1,0:T(8,128)} %bitcast.6), calls=%async_computation.1 | async-start | bytes 3145728 | tf_op jit(solution)/shard_map/all_to_all | solution.py:33
  187.8 35.4 %collective-permute-start = (bf16[16,1536]{1,0:T(8,128)(2,1)S(1)}, bf16[16,1536]{1,0:T(8,128)(2,1)S(1)}, u32[]{:S(2)}, u32[]{:S(2)}) collective-permute-start(bf16[16,1536]{1,0:T(8,128)(2,1)S(1)} %psum.49), channel_id=1, source_target_pairs={{0,32},{32,64},{64,96},{96,128},{128,160},{160,192},{192,224},{1,3... | collective-permute-start | bytes 147464 | tf_op jit(solution)/shard_map/ppermute | solution.py:10
  340.2 32.4 %collective-permute-start.1 = (bf16[16,1536]{1,0:T(8,128)(2,1)S(1)}, bf16[16,1536]{1,0:T(8,128)(2,1)S(1)}, u32[]{:S(2)}, u32[]{:S(2)}) collective-permute-start(bf16[16,1536]{1,0:T(8,128)(2,1)S(1)} %psum.50), channel_id=1, source_target_pairs={{0,32},{32,64},{64,96},{96,128},{128,160},{160,192},{192,224},{1,3... | collective-permute-start | bytes 147464 | tf_op jit(solution)/shard_map/ppermute | solution.py:10
  489.0 33.1 %collective-permute-start.2 = (bf16[16,1536]{1,0:T(8,128)(2,1)S(1)}, bf16[16,1536]{1,0:T(8,128)(2,1)S(1)}, u32[]{:S(2)}, u32[]{:S(2)}) collective-permute-start(bf16[16,1536]{1,0:T(8,128)(2,1)S(1)} %psum.51), channel_id=1, source_target_pairs={{0,32},{32,64},{64,96},{96,128},{128,160},{160,192},{192,224},{1,3... | collective-permute-start | bytes 147464 | tf_op jit(solution)/shard_map/ppermute | solution.py:10
  638.6 33.0 %collective-permute-start.3 = (bf16[16,1536]{1,0:T(8,128)(2,1)S(1)}, bf16[16,1536]{1,0:T(8,128)(2,1)S(1)}, u32[]{:S(2)}, u32[]{:S(2)}) collective-permute-start(bf16[16,1536]{1,0:T(8,128)(2,1)S(1)} %psum.52), channel_id=1, source_target_pairs={{0,32},{32,64},{64,96},{96,128},{128,160},{160,192},{192,224},{1,3... | collective-permute-start | bytes 147464 | tf_op jit(solution)/shard_map/ppermute | solution.py:10
  788.2 32.8 %collective-permute-start.4 = (bf16[16,1536]{1,0:T(8,128)(2,1)S(1)}, bf16[16,1536]{1,0:T(8,128)(2,1)S(1)}, u32[]{:S(2)}, u32[]{:S(2)}) collective-permute-start(bf16[16,1536]{1,0:T(8,128)(2,1)S(1)} %psum.53), channel_id=1, source_target_pairs={{0,32},{32,64},{64,96},{96,128},{128,160},{160,192},{192,224},{1,3... | collective-permute-start | bytes 147464 | tf_op jit(solution)/shard_map/ppermute | solution.py:10
  937.8 32.7 %collective-permute-start.5 = (bf16[16,1536]{1,0:T(8,128)(2,1)S(1)}, bf16[16,1536]{1,0:T(8,128)(2,1)S(1)}, u32[]{:S(2)}, u32[]{:S(2)}) collective-permute-start(bf16[16,1536]{1,0:T(8,128)(2,1)S(1)} %psum.54), channel_id=1, source_target_pairs={{0,32},{32,64},{64,96},{96,128},{128,160},{160,192},{192,224},{1,3... | collective-permute-start | bytes 147464 | tf_op jit(solution)/shard_map/ppermute | solution.py:10
  1087.4 32.5 %collective-permute-start.6 = (bf16[16,1536]{1,0:T(8,128)(2,1)S(1)}, bf16[16,1536]{1,0:T(8,128)(2,1)S(1)}, u32[]{:S(2)}, u32[]{:S(2)}) collective-permute-start(bf16[16,1536]{1,0:T(8,128)(2,1)S(1)} %psum.55), channel_id=1, source_target_pairs={{0,32},{32,64},{64,96},{96,128},{128,160},{160,192},{192,224},{1,3... | collective-permute-start | bytes 147464 | tf_op jit(solution)/shard_map/ppermute | solution.py:10
where the time goes:
time: 1130 us; the launch traced here: 1120 us
  blocking collectives  775 us (69%)
  starting transfers between devices  241 us (21%)
  matrix products  47.8 us (4%)
  waiting for transfers between devices  47.5 us (4%)
    psum x7, blocking collectives, on_device(): summed = lax.psum(panel_part, 'layer').astype(jnp.bfloat16)  775 us
    ppermute x7, starting transfers between devices, shifted(): return lax.ppermute(block, axis, route)  224 us
    all_to_all x1, waiting for transfers between devices, on_device(): lax.all_to_all(send_rows.reshape(group_size, capacity, face_width), 'laye...  35.1 us
    dot_general x8, matrix products, on_device(): jnp.einsum('rfw,fwv->rfv', local_part, inverse, preferred_element_type=jn...  25.7 us
  transfers between devices with their start and end apart: 9, of which 9 were waited for; matrix products, arithmetic and copies ran while one was open for 0% of the time, Pallas kernels for 0%

commit v1 on v0

--- a/solution.py
+++ b/solution.py
@@ -70,7 +70,7 @@
         solved = solve_solved
         panel_part = solve_panel_part
         if step_index + 1 < sections:
-            summed = lax.psum(panel_part, "layer").astype(jnp.bfloat16)
+            summed = lax.all_gather(panel_part, axis_name="layer").sum(axis=0).astype(jnp.bfloat16)
             arrived = shifted(summed, "sweep", 1)
             panel_in = arrived
     return solved[None]

time: 1130 us -> 729 us (0.65)
  blocking collectives: 775 us -> 0 us
  waiting for transfers between devices: 47.5 us -> 564 us
  starting transfers between devices: 241 us -> 70.2 us
  other arithmetic: 4.15 us -> 18.5 us
  between operations: 0.18 us -> 13.7 us
    psum x7 -> x0, blocking collectives: 775 us -> none  [on_device(): summed = lax.psum(panel_part, 'layer').astype(jnp.bfloat16)]
    all_gather x0 -> x7, waiting for transfers between devices: none -> 516 us  [on_device(): lax.all_gather(panel_part, axis_name='layer').sum(axis=0)]
    ppermute x7, starting transfers between devices: 224 us -> 53.3 us  [shifted(): return lax.ppermute(block, axis, route)]
    reduce_sum x0 -> x7, other arithmetic: none -> 14.3 us  [on_device(): lax.all_gather(panel_part, axis_name='layer').sum(axis=0)]
  transfers between devices with their start and end apart: 9 -> 16, of which waited for: 9 -> 16; matrix products, arithmetic and copies ran while one was open for 0% -> 1% of each run, Pallas kernels for 0% -> 0%
where the time goes in v1:
time: 729 us; the launch traced here: 727 us
  waiting for transfers between devices  564 us (77%)
  starting transfers between devices  70.2 us (10%)
  matrix products  52.4 us (7%)
  other arithmetic  18.5 us (3%)
  between operations  13.7 us (2%)
  local copies, waits for them, and re-layouts  8.93 us (1%)
    all_gather x7, waiting for transfers between devices, on_device(): lax.all_gather(panel_part, axis_name='layer').sum(axis=0)  516 us
    ppermute x7, starting transfers between devices, shifted(): return lax.ppermute(block, axis, route)  53.3 us
    all_to_all x1, waiting for transfers between devices, on_device(): lax.all_to_all(send_rows.reshape(group_size, capacity, face_width), 'laye...  35 us
    dot_general x7, matrix products, on_device(): jnp.dot(flattened, coupling_out, preferred_element_type=jnp.float32)  25.9 us
    dot_general x8, matrix products, on_device(): jnp.einsum('rfw,fwv->rfv', local_part, inverse, preferred_element_type=jn...  25.7 us
  transfers between devices with their start and end apart: 16, of which 16 were waited for; matrix products, arithmetic and copies ran while one was open for 1% of the time, Pallas kernels for 0%

profile of v1, /device:TPU:1, one launch (start us, length us, event | category | flops | bytes accessed | tf_op | source)
XLA Modules:
  0.0 727.5 jit_solution(15097511888904321015)
XLA Ops:
  7.3 1.2 reduce-window.6
  10.2 2.6 scatter_custom_fusion
  13.5 11.9 %all-to-all-start = ((s32[32,1,32]{2,1,0:T(1,128)}), s32[32,1,32]{2,1,0:T(1,128)S(1)}, u32[]{:S(2)}, u32[]{:S(2)}) async-start(s32[32,1,32]{2,1,0:T(1,128)} %all_to_all.9), calls=%async_computation | async-start | bytes 32768 | tf_op jit(solution)/shard_map/all_to_all | solution.py:40
  25.4 4.0 scatter_custom_fusion.1
  29.4 4.5 all-to-all-done
  33.9 4.7 all-to-all-start.1
  40.0 35.0 %all-to-all-done.1 = f32[32,32,384]{2,1,0:T(8,128)S(1)} async-done(((f32[32,32,384]{2,1,0:T(8,128)}), f32[32,32,384]{2,1,0:T(8,128)S(1)}, u32[]{:S(2)}, u32[]{:S(2)}) %all-to-all-start.1) | async-done | bytes 1572896 | tf_op jit(solution)/shard_map/all_to_all | solution.py:33
  75.7 3.2 fusion.136
  79.0 3.7 fusion.28
  82.7 76.5 %all-gather.15.cloned.1.call-done = f32[512,1536]{1,0:T(8,128)} async-done(((f32[16,1536]{1,0:T(8,128)}), f32[512,1536]{1,0:T(8,128)}) %all-gather.15.cloned.1.call-update) | async-done | bytes 3145744 | tf_op jit(solution)/shard_map/all_gather | solution.py:73
  159.2 2.0 reduce_sum.76
  161.3 7.6 %collective-permute-start = (bf16[16,1536]{1,0:T(8,128)(2,1)S(1)}, bf16[16,1536]{1,0:T(8,128)(2,1)S(1)}, u32[]{:S(2)}, u32[]{:S(2)}) collective-permute-start(bf16[16,1536]{1,0:T(8,128)(2,1)S(1)} %reduce_sum.76), channel_id=1, source_target_pairs={{0,32},{32,64},{64,96},{96,128},{128,160},{160,192},{192,224},{1,3... | collective-permute-start | bytes 147464 | tf_op jit(solution)/shard_map/ppermute | solution.py:10
  168.9 1.2 collective-permute-done
  170.0 3.2 fusion.133
  173.3 3.7 fusion.26
  177.0 73.3 %all-gather.17.cloned.1.call-done = f32[512,1536]{1,0:T(8,128)} async-done(((f32[16,1536]{1,0:T(8,128)}), f32[512,1536]{1,0:T(8,128)}) %all-gather.17.cloned.1.call-update) | async-done | bytes 3145744 | tf_op jit(solution)/shard_map/all_gather | solution.py:73
  250.3 2.0 reduce_sum.77
  252.4 7.6 %collective-permute-start.1 = (bf16[16,1536]{1,0:T(8,128)(2,1)S(1)}, bf16[16,1536]{1,0:T(8,128)(2,1)S(1)}, u32[]{:S(2)}, u32[]{:S(2)}) collective-permute-start(bf16[16,1536]{1,0:T(8,128)(2,1)S(1)} %reduce_sum.77), channel_id=1, source_target_pairs={{0,32},{32,64},{64,96},{96,128},{128,160},{160,192},{192,224},{1,3... | collective-permute-start | bytes 147464 | tf_op jit(solution)/shard_map/ppermute | solution.py:10
  260.0 1.2 collective-permute-done.1
  261.1 3.2 fusion.130
  264.4 3.7 fusion.24
  268.1 73.3 %all-gather.19.cloned.1.call-done = f32[512,1536]{1,0:T(8,128)} async-done(((f32[16,1536]{1,0:T(8,128)}), f32[512,1536]{1,0:T(8,128)}) %all-gather.19.cloned.1.call-update) | async-done | bytes 3145744 | tf_op jit(solution)/shard_map/all_gather | solution.py:73
  341.5 2.0 reduce_sum.78
  343.5 7.6 %collective-permute-start.2 = (bf16[16,1536]{1,0:T(8,128)(2,1)S(1)}, bf16[16,1536]{1,0:T(8,128)(2,1)S(1)}, u32[]{:S(2)}, u32[]{:S(2)}) collective-permute-start(bf16[16,1536]{1,0:T(8,128)(2,1)S(1)} %reduce_sum.78), channel_id=1, source_target_pairs={{0,32},{32,64},{64,96},{96,128},{128,160},{160,192},{192,224},{1,3... | collective-permute-start | bytes 147464 | tf_op jit(solution)/shard_map/ppermute | solution.py:10
  351.1 1.2 collective-permute-done.2
  352.2 3.2 fusion.127
  355.5 3.7 fusion.22
  359.3 73.3 %all-gather.21.cloned.1.call-done = f32[512,1536]{1,0:T(8,128)} async-done(((f32[16,1536]{1,0:T(8,128)}), f32[512,1536]{1,0:T(8,128)}) %all-gather.21.cloned.1.call-update) | async-done | bytes 3145744 | tf_op jit(solution)/shard_map/all_gather | solution.py:73
  432.6 2.0 reduce_sum.79
  434.6 7.8 %collective-permute-start.3 = (bf16[16,1536]{1,0:T(8,128)(2,1)S(1)}, bf16[16,1536]{1,0:T(8,128)(2,1)S(1)}, u32[]{:S(2)}, u32[]{:S(2)}) collective-permute-start(bf16[16,1536]{1,0:T(8,128)(2,1)S(1)} %reduce_sum.79), channel_id=1, source_target_pairs={{0,32},{32,64},{64,96},{96,128},{128,160},{160,192},{192,224},{1,3... | collective-permute-start | bytes 147464 | tf_op jit(solution)/shard_map/ppermute | solution.py:10
  443.4 3.2 fusion.124
  446.6 3.7 fusion.20
  450.4 73.3 %all-gather.23.cloned.1.call-done = f32[512,1536]{1,0:T(8,128)} async-done(((f32[16,1536]{1,0:T(8,128)}), f32[512,1536]{1,0:T(8,128)}) %all-gather.23.cloned.1.call-update) | async-done | bytes 3145744 | tf_op jit(solution)/shard_map/all_gather | solution.py:73
  523.7 2.0 reduce_sum.80
  525.7 7.6 %collective-permute-start.4 = (bf16[16,1536]{1,0:T(8,128)(2,1)S(1)}, bf16[16,1536]{1,0:T(8,128)(2,1)S(1)}, u32[]{:S(2)}, u32[]{:S(2)}) collective-permute-start(bf16[16,1536]{1,0:T(8,128)(2,1)S(1)} %reduce_sum.80), channel_id=1, source_target_pairs={{0,32},{32,64},{64,96},{96,128},{128,160},{160,192},{192,224},{1,3... | collective-permute-start | bytes 147464 | tf_op jit(solution)/shard_map/ppermute | solution.py:10
  533.3 1.2 collective-permute-done.4
  534.5 3.2 fusion.121
  537.7 3.7 fusion.18
  541.5 73.3 %all-gather.25.cloned.1.call-done = f32[512,1536]{1,0:T(8,128)} async-done(((f32[16,1536]{1,0:T(8,128)}), f32[512,1536]{1,0:T(8,128)}) %all-gather.25.cloned.1.call-update) | async-done | bytes 3145744 | tf_op jit(solution)/shard_map/all_gather | solution.py:73
  614.8 2.0 reduce_sum.81
  616.9 7.6 %collective-permute-start.5 = (bf16[16,1536]{1,0:T(8,128)(2,1)S(1)}, bf16[16,1536]{1,0:T(8,128)(2,1)S(1)}, u32[]{:S(2)}, u32[]{:S(2)}) collective-permute-start(bf16[16,1536]{1,0:T(8,128)(2,1)S(1)} %reduce_sum.81), channel_id=1, source_target_pairs={{0,32},{32,64},{64,96},{96,128},{128,160},{160,192},{192,224},{1,3... | collective-permute-start | bytes 147464 | tf_op jit(solution)/shard_map/ppermute | solution.py:10
  624.4 1.2 collective-permute-done.5
  625.6 3.2 fusion.118
  628.8 3.7 fusion.16
  632.6 73.4 %all-gather.27.cloned.1.call-done = f32[512,1536]{1,0:T(8,128)} async-done(((f32[16,1536]{1,0:T(8,128)}), f32[512,1536]{1,0:T(8,128)}) %all-gather.27.cloned.1.call-update) | async-done | bytes 3145744 | tf_op jit(solution)/shard_map/all_gather | solution.py:73
  705.9 2.0 reduce_sum.82
  708.0 7.6 %collective-permute-start.6 = (bf16[16,1536]{1,0:T(8,128)(2,1)S(1)}, bf16[16,1536]{1,0:T(8,128)(2,1)S(1)}, u32[]{:S(2)}, u32[]{:S(2)}) collective-permute-start(bf16[16,1536]{1,0:T(8,128)(2,1)S(1)} %reduce_sum.82), channel_id=1, source_target_pairs={{0,32},{32,64},{64,96},{96,128},{128,160},{160,192},{192,224},{1,3... | collective-permute-start | bytes 147464 | tf_op jit(solution)/shard_map/ppermute | solution.py:10
  716.7 3.2 fusion.46
  (40 shorter events, 8.5 us)
Async XLA Ops:
  6.5 69.2 %copy-start = (bf16[1,4,384,384]{3,2,1,0:T(8,128)(2,1)S(1)}, bf16[1,4,384,384]{3,2,1,0:T(8,128)(2,1)}, u32[]{:S(2)}) copy-start(bf16[1,4,384,384]{3,2,1,0:T(8,128)(2,1)} %param.11) | copy-start | bytes 3538948
  6.5 68.5 %copy-start.1 = (f32[1,16,4,384]{3,2,1,0:T(4,128)S(1)}, f32[1,16,4,384]{3,2,1,0:T(4,128)}, u32[]{:S(2)}) copy-start(f32[1,16,4,384]{3,2,1,0:T(4,128)} %param.7) | copy-start | bytes 294916
  13.5 20.4 %all-to-all-start = ((s32[32,1,32]{2,1,0:T(1,128)}), s32[32,1,32]{2,1,0:T(1,128)S(1)}, u32[]{:S(2)}, u32[]{:S(2)}) async-start(s32[32,1,32]{2,1,0:T(1,128)} %all_to_all.9), calls=%async_computation | async-start | bytes 32768 | tf_op jit(solution)/shard_map/all_to_all | solution.py:40
  33.9 41.1 %all-to-all-start.1 = ((f32[32,32,384]{2,1,0:T(8,128)}), f32[32,32,384]{2,1,0:T(8,128)S(1)}, u32[]{:S(2)}, u32[]{:S(2)}) async-start(f32[32,32,384]{2,1,0:T(8,128)} %bitcast.6), calls=%async_computation.1 | async-start | bytes 3145728 | tf_op jit(solution)/shard_map/all_to_all | solution.py:33
  38.7 120.6 %all-gather.15.cloned.1.call-start = ((), (), s32[]{:S(2)}) async-start(), calls=%async_computation.2 | async-start | bytes 3244032 | tf_op jit(solution)/shard_map/all_gather | solution.py:73
  82.7 167.6 %all-gather.17.cloned.1.call-start = ((), (), s32[]{:S(2)}) async-start(), calls=%async_computation.3 | async-start | bytes 3244032 | tf_op jit(solution)/shard_map/all_gather | solution.py:73
  161.3 8.7 %collective-permute-start = (bf16[16,1536]{1,0:T(8,128)(2,1)S(1)}, bf16[16,1536]{1,0:T(8,128)(2,1)S(1)}, u32[]{:S(2)}, u32[]{:S(2)}) collective-permute-start(bf16[16,1536]{1,0:T(8,128)(2,1)S(1)} %reduce_sum.76), channel_id=1, source_target_pairs={{0,32},{32,64},{64,96},{96,128},{128,160},{160,192},{192,224},{1,3... | collective-permute-start | bytes 147464 | tf_op jit(solution)/shard_map/ppermute | solution.py:10
  177.0 164.5 %all-gather.19.cloned.1.call-start = ((), (), s32[]{:S(2)}) async-start(), calls=%async_computation.4 | async-start | bytes 3244032 | tf_op jit(solution)/shard_map/all_gather | solution.py:73
  252.4 8.7 %collective-permute-start.1 = (bf16[16,1536]{1,0:T(8,128)(2,1)S(1)}, bf16[16,1536]{1,0:T(8,128)(2,1)S(1)}, u32[]{:S(2)}, u32[]{:S(2)}) collective-permute-start(bf16[16,1536]{1,0:T(8,128)(2,1)S(1)} %reduce_sum.77), channel_id=1, source_target_pairs={{0,32},{32,64},{64,96},{96,128},{128,160},{160,192},{192,224},{1,3... | collective-permute-start | bytes 147464 | tf_op jit(solution)/shard_map/ppermute | solution.py:10
  268.1 164.5 %all-gather.21.cloned.1.call-start = ((), (), s32[]{:S(2)}) async-start(), calls=%async_computation.5 | async-start | bytes 3244032 | tf_op jit(solution)/shard_map/all_gather | solution.py:73
  343.5 8.7 %collective-permute-start.2 = (bf16[16,1536]{1,0:T(8,128)(2,1)S(1)}, bf16[16,1536]{1,0:T(8,128)(2,1)S(1)}, u32[]{:S(2)}, u32[]{:S(2)}) collective-permute-start(bf16[16,1536]{1,0:T(8,128)(2,1)S(1)} %reduce_sum.78), channel_id=1, source_target_pairs={{0,32},{32,64},{64,96},{96,128},{128,160},{160,192},{192,224},{1,3... | collective-permute-start | bytes 147464 | tf_op jit(solution)/shard_map/ppermute | solution.py:10
  359.2 164.5 %all-gather.23.cloned.1.call-start = ((), (), s32[]{:S(2)}) async-start(), calls=%async_computation.6 | async-start | bytes 3244032 | tf_op jit(solution)/shard_map/all_gather | solution.py:73
  434.6 8.7 %collective-permute-start.3 = (bf16[16,1536]{1,0:T(8,128)(2,1)S(1)}, bf16[16,1536]{1,0:T(8,128)(2,1)S(1)}, u32[]{:S(2)}, u32[]{:S(2)}) collective-permute-start(bf16[16,1536]{1,0:T(8,128)(2,1)S(1)} %reduce_sum.79), channel_id=1, source_target_pairs={{0,32},{32,64},{64,96},{96,128},{128,160},{160,192},{192,224},{1,3... | collective-permute-start | bytes 147464 | tf_op jit(solution)/shard_map/ppermute | solution.py:10
  450.3 164.5 %all-gather.25.cloned.1.call-start = ((), (), s32[]{:S(2)}) async-start(), calls=%async_computation.7 | async-start | bytes 3244032 | tf_op jit(solution)/shard_map/all_gather | solution.py:73
  525.7 8.7 %collective-permute-start.4 = (bf16[16,1536]{1,0:T(8,128)(2,1)S(1)}, bf16[16,1536]{1,0:T(8,128)(2,1)S(1)}, u32[]{:S(2)}, u32[]{:S(2)}) collective-permute-start(bf16[16,1536]{1,0:T(8,128)(2,1)S(1)} %reduce_sum.80), channel_id=1, source_target_pairs={{0,32},{32,64},{64,96},{96,128},{128,160},{160,192},{192,224},{1,3... | collective-permute-start | bytes 147464 | tf_op jit(solution)/shard_map/ppermute | solution.py:10
  541.5 164.5 %all-gather.27.cloned.1.call-start = ((), (), s32[]{:S(2)}) async-start(), calls=%async_computation.8 | async-start | bytes 3244032 | tf_op jit(solution)/shard_map/all_gather | solution.py:73
  616.9 8.7 %collective-permute-start.5 = (bf16[16,1536]{1,0:T(8,128)(2,1)S(1)}, bf16[16,1536]{1,0:T(8,128)(2,1)S(1)}, u32[]{:S(2)}, u32[]{:S(2)}) collective-permute-start(bf16[16,1536]{1,0:T(8,128)(2,1)S(1)} %reduce_sum.81), channel_id=1, source_target_pairs={{0,32},{32,64},{64,96},{96,128},{128,160},{160,192},{192,224},{1,3... | collective-permute-start | bytes 147464 | tf_op jit(solution)/shard_map/ppermute | solution.py:10
  708.0 8.7 %collective-permute-start.6 = (bf16[16,1536]{1,0:T(8,128)(2,1)S(1)}, bf16[16,1536]{1,0:T(8,128)(2,1)S(1)}, u32[]{:S(2)}, u32[]{:S(2)}) collective-permute-start(bf16[16,1536]{1,0:T(8,128)(2,1)S(1)} %reduce_sum.82), channel_id=1, source_target_pairs={{0,32},{32,64},{64,96},{96,128},{128,160},{160,192},{192,224},{1,3... | collective-permute-start | bytes 147464 | tf_op jit(solution)/shard_map/ppermute | solution.py:10
Sparse Core Ops, SparseCore 0:
  82.8 76.3 all-gather.14
  177.1 73.1 all-gather.16
  268.2 73.1 all-gather.18
  359.3 73.1 all-gather.20
  450.5 73.1 all-gather.22
  541.6 73.1 all-gather.24
  632.7 73.1 all-gather.26
